TPU v7x, 128 devices: a whole 4x4x4 slice. The times are simulated.
128 devices in a mesh: query: 4 (over z_lo, core), lib: 32 (over x, y, z_hi).
Axes of the slice: x: 4, y: 4, z: 4 (z_hi: 2, z_lo: 2; z = z_hi * 2 + z_lo), core: 2. Of those that a mesh axis runs over, the one named last changes fastest.
Arguments:
- queries: bfloat16 [4096, 2048], P(('query', 'lib')), may hold values from -64 to 64
- query_bucket: int32 [4096], P(('query', 'lib')), may hold values from 0 to 63, as said below
- library: bfloat16 [98304, 2048], P(('lib', 'query')), may hold values from -64 to 64
- library_time: bfloat16 [98304], P(('lib', 'query')), may hold values from 0 to 2
- library_bucket: int32 [98304], P(('lib', 'query')), may hold values from 0 to 63, as said below
Outputs:
- expected_spectra: bfloat16 [4096, 2048], P(('query', 'lib'))
- expected_time: float32 [4096], P(('query', 'lib'))
- log_evidence: float32 [4096], P(('query', 'lib'))
Inputs may be any that keep to these rules, and one draw needn't show every extreme that they name: `query_bucket`: library entries whose bucket differs from a query's by at most one are that query's candidates; the queries held by the devices at index i of lib lie in buckets 2 i and 2 i + 1. `library_bucket`: the library entries of every device hold each of the 64 buckets exactly 3072 // 256 times.
All inputs are finite; a program needn't handle non-finite values.
Results may differ from a plain program's by a relative error of at most 0.003.
Values may be sent and summed in bfloat16 or wider, within the bound.
A program may use at most 128 MiB of HBM per device.

v0:
```python
import jax
import jax.numpy as jnp
from jax import lax
from jax.sharding import PartitionSpec as P

SHARPNESS = 448
PER_BUCKET = 12
N_LIB = 32


def entry_scale(spectra_rows):
    return lax.rsqrt(jnp.mean(jnp.square(spectra_rows.astype(jnp.float32)), axis=1) + 1e-06)


def bucket_positions(bucket):
    n = bucket.shape[0]
    at = jnp.arange(n)
    same = (bucket[None, :] == bucket[:, None]) & (at[None, :] < at[:, None])
    rank = jnp.sum(same.astype(jnp.int32), axis=1)
    return bucket * PER_BUCKET + rank


def per_device(queries, query_bucket, library, library_time, library_bucket):
    own_rows, bin_count = queries.shape
    lib_at = lax.axis_index("lib")
    positions = bucket_positions(library_bucket)
    row = jnp.arange(N_LIB * 48)
    wanted = row // 48 * 24 - 12 + row % 48
    pick = (wanted[:, None] == positions[None, :]).astype(jnp.bfloat16)
    send = jnp.dot(pick, library, preferred_element_type=jnp.float32).astype(jnp.bfloat16)
    send_time = jnp.dot(pick, library_time, preferred_element_type=jnp.float32).astype(jnp.bfloat16)
    entries = lax.all_to_all(send.reshape(N_LIB, 48, bin_count), "lib", 0, 0).reshape(
        N_LIB * 48, bin_count
    )
    entry_time = lax.all_to_all(send_time.reshape(N_LIB, 48), "lib", 0, 0).reshape(N_LIB * 48)
    query_block = lax.all_gather(queries, "query", axis=0, tiled=True)
    block_bucket = lax.all_gather(query_bucket, "query", axis=0, tiled=True)
    query_scale = entry_scale(query_block) * (SHARPNESS / bin_count)
    products = lax.dot_general(
        query_block, entries, (((1,), (1,)), ((), ())), preferred_element_type=jnp.float32
    )
    row_bucket = 2 * lib_at - 1 + row % 48 // PER_BUCKET
    inside = jnp.abs(block_bucket[:, None] - row_bucket[None, :]) <= 1
    inside = inside & (row_bucket >= 0)[None, :] & (row_bucket < 2 * N_LIB)[None, :]
    scores = jnp.where(
        inside, products * query_scale[:, None] * entry_scale(entries)[None, :], -jnp.inf
    )
    maxima = lax.pmax(jnp.max(scores, axis=1), "query")
    weights = jnp.exp(scores - maxima[:, None]).astype(jnp.bfloat16)
    total_part = jnp.sum(weights.astype(jnp.float32), axis=1)
    spectra_part = jnp.dot(weights, entries, preferred_element_type=jnp.float32)
    time_part = jnp.dot(weights, entry_time, preferred_element_type=jnp.float32)
    total_all, time_all = lax.psum((total_part, time_part), "query")
    spectra_sum = lax.psum_scatter(spectra_part, "query", scatter_dimension=0, tiled=True)
    first_row = lax.axis_index("query") * own_rows
    totals = lax.dynamic_slice_in_dim(total_all, first_row, own_rows)
    time_sum = lax.dynamic_slice_in_dim(time_all, first_row, own_rows)
    own_maxima = lax.dynamic_slice_in_dim(maxima, first_row, own_rows)
    expected = (spectra_sum / totals[:, None]).astype(jnp.bfloat16)
    return (expected, time_sum / totals, own_maxima + jnp.log(totals))


def solution(mesh):
    placed = (
        P(("query", "lib"), None),
        P(("query", "lib")),
        P(("lib", "query"), None),
        P(("lib", "query")),
        P(("lib", "query")),
    )
    return jax.shard_map(
        per_device,
        mesh=mesh,
        in_specs=placed,
        out_specs=(P(("query", "lib"), None), P(("query", "lib")), P(("query", "lib"))),
        check_vma=False,
    )
```

profile of v0, /device:TPU:1, one launch (start us, length us, event | category | flops | bytes accessed | tf_op | source)
XLA Modules:
  0.0 188.5 jit_solution(15114478839216429072)
XLA Ops:
  7.2 1.2 convert_reduce_fusion
  8.4 0.7 multiply_add_fusion
  9.1 7.1 %convolution_convert_fusion = bf16[1536,2048]{1,0:T(8,128)(2,1)} fusion(bf16[768,2048]{1,0:T(8,128)(2,1)S(1)} %copy-done, s32[768]{0:T(1024)S(1)} %multiply_add_fusion, s32[1536]{0:T(1024)S(1)} %fusion.18), kind=kOutput, calls=%fused_computation.1 | convolution fusion | flops 4836163584 | bytes 9446400 | tf_op jit(solution)/shard_map/dot_general | solution.py:30
  16.2 11.4 %all-to-all-start = ((bf16[32,48,2048]{2,1,0:T(8,128)(2,1)}), bf16[32,48,2048]{2,1,0:T(8,128)(2,1)}, u32[]{:S(2)}, u32[]{:S(2)}) async-start(bf16[32,48,2048]{2,1,0:T(8,128)(2,1)} %bitcast.17), calls=%async_computation | async-start | bytes 12582912 | tf_op jit(solution)/shard_map/all_to_all | solution.py:32
  27.7 0.6 dynamic-slice
  29.2 24.7 %all-reduce = s32[128]{0:T(128)S(1)} all-reduce(s32[128]{0:T(128)S(1)} %dynamic-update-slice), channel_id=1, replica_groups=mesh['query'=4,'lib'=32] {'query'}, use_global_device_ids=true, to_apply=%add | all-reduce | flops 128 | bytes 1024
  54.0 17.4 %all_gather.7 = bf16[128,2048]{1,0:T(8,128)(2,1)S(1)} all-gather(bf16[32,2048]{1,0:T(8,128)(2,1)S(1)} %copy-done.2), channel_id=1, replica_groups=mesh['query'=4,'lib'=32] {'query'}, dimensions={0}, use_global_device_ids=true | all-gather | bytes 655360 | tf_op jit(solution)/shard_map/all_gather | solution.py:36
  71.4 0.8 copy-done.1
  72.4 55.2 %all-to-all-done = bf16[32,48,2048]{2,1,0:T(8,128)(2,1)} async-done(((bf16[32,48,2048]{2,1,0:T(8,128)(2,1)}), bf16[32,48,2048]{2,1,0:T(8,128)(2,1)}, u32[]{:S(2)}, u32[]{:S(2)}) %all-to-all-start) | async-done | bytes 6291488 | tf_op jit(solution)/shard_map/all_to_all | solution.py:32
  127.6 4.1 %multiply_reduce_fusion = f32[32,48]{1,0:T(8,128)S(1)} fusion(bf16[32,48,2048]{2,1,0:T(8,128)(2,1)} %all-to-all-done), kind=kLoop, calls=%fused_computation | loop fusion | flops 9435648 | bytes 6297600 | tf_op jit(solution)/shard_map/reduce_sum | solution.py:12
  131.7 5.0 %fusion.26 = (f32[128]{0:T(128)S(1)}, f32[128,1536]{0,1:T(8,128)}) fusion(f32[1536]{0:T(1024)S(1)} %rsqrt.19, f32[128]{0:T(128)S(1)} %rsqrt_multiply_fusion, bf16[1536,2048]{1,0:T(8,128)(2,1)} %bitcast.2, bf16[128,2048]{1,0:T(8,128)(2,1)} %copy-done.1, pred[1536]{0:T(1024)(128)(4,1)S(1)} %get-tuple-element.11, pred[1536]{0:T(1024)(128)(4,1)S(1)} %get-tuple-element.12, ...), kind=kOutput, calls=%fused_computation.50 | convolution fusion | flops 807075712 | bytes 7619072 | tf_op jit(solution)/shard_map/dot_general | solution.py:39
  136.7 8.2 %pmax.7 = f32[128]{0:T(128)S(1)} all-reduce(f32[128]{0:T(128)S(1)} %get-tuple-element.9), channel_id=1, replica_groups=mesh['query'=4,'lib'=32] {'query'}, use_global_device_ids=true, to_apply=%region_4.5 | all-reduce | flops 128 | bytes 1024 | tf_op jit(solution)/shard_map/pmax | solution.py:48
  144.9 1.9 convert_reduce_fusion.1
  146.8 4.8 %fusion.27 = f32[128,2048]{1,0:T(8,128)} fusion(bf16[128,1536]{0,1:T(8,128)(2,1)S(1)} %get-tuple-element.8, bf16[1536,2048]{1,0:T(8,128)(2,1)} %bitcast.2), kind=kOutput, calls=%fused_computation.51 | convolution fusion | flops 805306368 | bytes 7733248 | tf_op jit(solution)/shard_map/dot_general | solution.py:51
  151.6 0.7 reshape.98
  152.3 0.9 fusion.11
  153.2 0.7 all_to_all.12
  153.9 6.9 %all-to-all-start.1 = ((bf16[32,1,48]{2,1,0:T(2,128)(2,1)}), bf16[32,1,48]{2,1,0:T(2,128)(2,1)S(1)}, u32[]{:S(2)}, u32[]{:S(2)}) async-start(bf16[32,1,48]{2,1,0:T(2,128)(2,1)} %all_to_all.12), calls=%async_computation.2 | async-start | bytes 32768 | tf_op jit(solution)/shard_map/all_to_all | solution.py:35
  160.8 8.5 %all-to-all-done.1 = bf16[32,1,48]{2,1,0:T(2,128)(2,1)S(1)} async-done(((bf16[32,1,48]{2,1,0:T(2,128)(2,1)}), bf16[32,1,48]{2,1,0:T(2,128)(2,1)S(1)}, u32[]{:S(2)}, u32[]{:S(2)}) %all-to-all-start.1) | async-done | bytes 3104 | tf_op jit(solution)/shard_map/all_to_all | solution.py:35
  169.3 0.7 reduce.2
  170.0 0.8 reshape.100
  170.9 7.2 %all-reduce.1 = (f32[128]{0:T(128)S(1)}, f32[128]{0:T(128)S(1)}) all-reduce(f32[128]{0:T(128)} %get-tuple-element.7, f32[128]{0:T(128)S(1)} %convolution_bitcast_fusion), channel_id=1, replica_groups=mesh['query'=4,'lib'=32] {'query'}, use_global_device_ids=true, to_apply=%region_7.8 | all-reduce | flops 256 | bytes 2048 | tf_op jit(solution)/shard_map/psum | solution.py:53
  178.1 1.3 log_add_fusion
  180.0 1.7 divide_convert_fusion
  (25 shorter events, 1.4 us)
Async XLA Ops:
  7.2 1.9 %copy-start = (bf16[768,2048]{1,0:T(8,128)(2,1)S(1)}, bf16[768,2048]{1,0:T(8,128)(2,1)}, u32[]{:S(2)}) copy-start(bf16[768,2048]{1,0:T(8,128)(2,1)} %param.7) | copy-start | bytes 9437188
  16.2 11.5 %copy-start.5 = (u32[128]{0:T(128)S(1)}, u32[128]{0:T(128)}, u32[]{:S(2)}) copy-start(u32[128]{0:T(128)} %constant.75) | copy-start | bytes 1540
  16.2 12.7 %copy-start.4 = (s32[32]{0:T(128)S(1)}, s32[32]{0:T(128)}, u32[]{:S(2)}) copy-start(s32[32]{0:T(128)} %param.6) | copy-start | bytes 388
  16.2 37.7 %copy-start.2 = (bf16[32,2048]{1,0:T(8,128)(2,1)S(1)}, bf16[32,2048]{1,0:T(8,128)(2,1)}, u32[]{:S(2)}) copy-start(bf16[32,2048]{1,0:T(8,128)(2,1)} %param.5) | copy-start | bytes 393220
  16.2 111.4 %all-to-all-start = ((bf16[32,48,2048]{2,1,0:T(8,128)(2,1)}), bf16[32,48,2048]{2,1,0:T(8,128)(2,1)}, u32[]{:S(2)}, u32[]{:S(2)}) async-start(bf16[32,48,2048]{2,1,0:T(8,128)(2,1)} %bitcast.17), calls=%async_computation | async-start | bytes 12582912 | tf_op jit(solution)/shard_map/all_to_all | solution.py:32
  27.7 152.3 %reduce-scatter.2.cloned.1.call-start = ((), (), s32[]{:S(2)}) async-start(), calls=%async_computation.3 | async-start | bytes 1310720 | tf_op jit(solution)/shard_map/reduce_scatter | solution.py:54
  71.4 0.8 copy-start.1
  144.9 6.7 %copy-start.3 = (f32[128]{0:T(128)}, f32[128]{0:T(128)S(1)}, u32[]{:S(2)}) copy-start(f32[128]{0:T(128)S(1)} %pmax.7) | copy-start | bytes 1540
  153.9 15.4 %all-to-all-start.1 = ((bf16[32,1,48]{2,1,0:T(2,128)(2,1)}), bf16[32,1,48]{2,1,0:T(2,128)(2,1)S(1)}, u32[]{:S(2)}, u32[]{:S(2)}) async-start(bf16[32,1,48]{2,1,0:T(2,128)(2,1)} %all_to_all.12), calls=%async_computation.2 | async-start | bytes 32768 | tf_op jit(solution)/shard_map/all_to_all | solution.py:35
Sparse Core Ops, SparseCore 0:
  151.8 19.7 reduce-scatter.1
where the time goes:
time: 189 us
  waiting for transfers between devices  63.8 us (34%)
  blocking collectives  57.5 us (30%)
  starting transfers between devices  18.3 us (10%)
  matrix products  18 us (10%)
  between operations  14.8 us (8%)
  other arithmetic  12.3 us (7%)
  local copies, waits for them, and re-layouts  3.92 us (2%)
    all_to_all x1, waiting for transfers between devices, per_device(): lax.all_to_all(send.reshape(N_LIB, 48, bin_count), 'lib', 0, 0)  55.2 us
    unnamed x1, blocking collectives  24.7 us
    all_gather x1, blocking collectives, per_device(): query_block = lax.all_gather(queries, 'query', axis=0, tiled=True)  17.4 us
    all_to_all x1, starting transfers between devices, per_device(): lax.all_to_all(send.reshape(N_LIB, 48, bin_count), 'lib', 0, 0)  11.4 us
    all_to_all x1, waiting for transfers between devices, per_device(): lax.all_to_all(send_time.reshape(N_LIB, 48), 'lib', 0, 0)  8.54 us
    pmax x1, blocking collectives, per_device(): maxima = lax.pmax(jnp.max(scores, axis=1), 'query')  8.21 us
    psum x1, blocking collectives, per_device(): total_all, time_all = lax.psum((total_part, time_part), 'query')  7.2 us
    dot_general x1, matrix products, per_device(): jnp.dot(pick, library, preferred_element_type=jnp.float32)  7.11 us
  transfers between devices with their start and end apart: 3, of which 2 were waited for; matrix products, arithmetic and copies ran while one was open for 3% of the time, Pallas kernels for 0%

commit v1 on v0

--- a/solution.py
+++ b/solution.py
@@ -33,7 +33,10 @@
         N_LIB * 48, bin_count
     )
     entry_time = lax.all_to_all(send_time.reshape(N_LIB, 48), "lib", 0, 0).reshape(N_LIB * 48)
-    query_block = lax.all_gather(queries, "query", axis=0, tiled=True)
+    count = lax.axis_size("query")
+    blocks = jnp.stack([queries for _ in range(count)])
+    blocks = lax.all_to_all(blocks, "query", split_axis=0, concat_axis=0)
+    query_block = jnp.concatenate(blocks, axis=0)
     block_bucket = lax.all_gather(query_bucket, "query", axis=0, tiled=True)
     query_scale = entry_scale(query_block) * (SHARPNESS / bin_count)
     products = lax.dot_general(

time: 189 us -> 202 us (1.069)
  waiting for transfers between devices: 63.8 us -> 87.4 us
  blocking collectives: 57.5 us -> 39.1 us
  starting transfers between devices: 18.3 us -> 23.7 us
    all_to_all x1, waiting for transfers between devices: 55.2 us -> 78.8 us  [per_device(): lax.all_to_all(send.reshape(N_LIB, 48, bin_count), 'lib', 0, 0)]
    all_gather x1 -> x0, blocking collectives: 17.4 us -> none  [per_device(): query_block = lax.all_gather(queries, 'query', axis=0, tiled=True)]
    all_to_all x0 -> x1, starting transfers between devices: none -> 5.48 us  [per_device(): blocks = lax.all_to_all(blocks, 'query', split_axis=0, concat_axis=0)]
  transfers between devices with their start and end apart: 3 -> 4, of which waited for: 2 -> 2; matrix products, arithmetic and copies ran while one was open for 3% -> 8% of each run, Pallas kernels for 0% -> 0%
where the time goes in v1:
time: 202 us; the launch traced here: 201 us
  waiting for transfers between devices  87.4 us (43%)
  blocking collectives  39.1 us (19%)
  starting transfers between devices  23.7 us (12%)
  matrix products  17.9 us (9%)
  between operations  14.8 us (7%)
  other arithmetic  13.3 us (7%)
  local copies, waits for them, and re-layouts  5.07 us (3%)
    all_to_all x1, waiting for transfers between devices, per_device(): lax.all_to_all(send.reshape(N_LIB, 48, bin_count), 'lib', 0, 0)  78.8 us
    unnamed x1, blocking collectives  25 us
    all_to_all x1, starting transfers between devices, per_device(): lax.all_to_all(send.reshape(N_LIB, 48, bin_count), 'lib', 0, 0)  10.7 us
    all_to_all x1, waiting for transfers between devices, per_device(): lax.all_to_all(send_time.reshape(N_LIB, 48), 'lib', 0, 0)  8.54 us
    all_to_all x1, starting transfers between devices, per_device(): lax.all_to_all(send_time.reshape(N_LIB, 48), 'lib', 0, 0)  7.48 us
    psum x1, blocking collectives, per_device(): total_all, time_all = lax.psum((total_part, time_part), 'query')  7.2 us
    dot_general x1, matrix products, per_device(): jnp.dot(pick, library, preferred_element_type=jnp.float32)  7.11 us
    pmax x1, blocking collectives, per_device(): maxima = lax.pmax(jnp.max(scores, axis=1), 'query')  6.97 us
  transfers between devices with their start and end apart: 4, of which 2 were waited for; matrix products, arithmetic and copies ran while one was open for 8% of the time, Pallas kernels for 0%

profile of v1, /device:TPU:1, one launch (start us, length us, event | category | flops | bytes accessed | tf_op | source)
XLA Modules:
  0.0 201.3 jit_solution(13928245401760167857)
XLA Ops:
  7.2 1.9 stack.2
  9.1 5.5 %all-to-all-start.1 = ((bf16[4,32,2048]{2,1,0:T(8,128)(2,1)}), bf16[4,32,2048]{2,1,0:T(8,128)(2,1)}, u32[]{:S(2)}, u32[]{:S(2)}) async-start(bf16[4,32,2048]{2,1,0:T(8,128)(2,1)} %stack.2), calls=%async_computation.1 | async-start | bytes 1048576 | tf_op jit(solution)/shard_map/all_to_all | solution.py:38
  14.6 1.1 convert_reduce_fusion
  15.7 0.7 multiply_add_fusion
  16.4 7.1 %convolution_convert_fusion = bf16[1536,2048]{1,0:T(8,128)(2,1)} fusion(bf16[768,2048]{1,0:T(8,128)(2,1)S(1)} %copy-done, s32[768]{0:T(1024)S(1)} %multiply_add_fusion, s32[1536]{0:T(1024)S(1)} %fusion.18), kind=kOutput, calls=%fused_computation.1 | convolution fusion | flops 4836163584 | bytes 9446400 | tf_op jit(solution)/shard_map/dot_general | solution.py:30
  23.5 10.7 %all-to-all-start = ((bf16[32,48,2048]{2,1,0:T(8,128)(2,1)}), bf16[32,48,2048]{2,1,0:T(8,128)(2,1)}, u32[]{:S(2)}, u32[]{:S(2)}) async-start(bf16[32,48,2048]{2,1,0:T(8,128)(2,1)} %bitcast.18), calls=%async_computation | async-start | bytes 12582912 | tf_op jit(solution)/shard_map/all_to_all | solution.py:32
  35.8 25.0 %all-reduce = s32[128]{0:T(128)S(1)} all-reduce(s32[128]{0:T(128)S(1)} %dynamic-update-slice), channel_id=1, replica_groups=mesh['query'=4,'lib'=32] {'query'}, use_global_device_ids=true, to_apply=%add | all-reduce | flops 128 | bytes 1024
  60.8 1.2 multiply_reduce_fusion.1
  62.1 78.8 %all-to-all-done = bf16[32,48,2048]{2,1,0:T(8,128)(2,1)} async-done(((bf16[32,48,2048]{2,1,0:T(8,128)(2,1)}), bf16[32,48,2048]{2,1,0:T(8,128)(2,1)}, u32[]{:S(2)}, u32[]{:S(2)}) %all-to-all-start) | async-done | bytes 6291488 | tf_op jit(solution)/shard_map/all_to_all | solution.py:32
  141.0 4.1 %multiply_reduce_fusion = f32[32,48]{1,0:T(8,128)S(1)} fusion(bf16[32,48,2048]{2,1,0:T(8,128)(2,1)} %all-to-all-done), kind=kLoop, calls=%fused_computation | loop fusion | flops 9435648 | bytes 6297600 | tf_op jit(solution)/shard_map/reduce_sum | solution.py:12
  145.1 5.0 %fusion.26 = (f32[128]{0:T(128)S(1)}, f32[128,1536]{0,1:T(8,128)}) fusion(f32[1536]{0:T(1024)S(1)} %rsqrt.20, f32[128]{0:T(128)S(1)} %mul.58, bf16[1536,2048]{1,0:T(8,128)(2,1)} %bitcast.2, bf16[128,2048]{1,0:T(8,128)(2,1)} %bitcast.3, pred[1536]{0:T(1024)(128)(4,1)S(1)} %get-tuple-element.11, pred[1536]{0:T(1024)(128)(4,1)S(1)} %get-tuple-element.12, ...), kind=kOutput, calls=%fused_computation.50 | convolution fusion | flops 807075712 | bytes 7619072 | tf_op jit(solution)/shard_map/dot_general | solution.py:42
  150.1 7.0 %pmax.7 = f32[128]{0:T(128)S(1)} all-reduce(f32[128]{0:T(128)S(1)} %get-tuple-element.9), channel_id=1, replica_groups=mesh['query'=4,'lib'=32] {'query'}, use_global_device_ids=true, to_apply=%region_4.5 | all-reduce | flops 128 | bytes 1024 | tf_op jit(solution)/shard_map/pmax | solution.py:51
  157.1 1.9 convert_reduce_fusion.1
  159.0 4.8 %fusion.27 = f32[128,2048]{1,0:T(8,128)} fusion(bf16[128,1536]{0,1:T(8,128)(2,1)S(1)} %get-tuple-element.8, bf16[1536,2048]{1,0:T(8,128)(2,1)} %bitcast.2), kind=kOutput, calls=%fused_computation.51 | convolution fusion | flops 805306368 | bytes 7733248 | tf_op jit(solution)/shard_map/dot_general | solution.py:54
  163.8 0.7 reshape.115
  164.5 0.9 fusion.11
  165.4 0.7 all_to_all.16
  166.1 7.5 %all-to-all-start.2 = ((bf16[32,1,48]{2,1,0:T(2,128)(2,1)}), bf16[32,1,48]{2,1,0:T(2,128)(2,1)S(1)}, u32[]{:S(2)}, u32[]{:S(2)}) async-start(bf16[32,1,48]{2,1,0:T(2,128)(2,1)} %all_to_all.16), calls=%async_computation.3 | async-start | bytes 32768 | tf_op jit(solution)/shard_map/all_to_all | solution.py:35
  173.6 8.5 %all-to-all-done.2 = bf16[32,1,48]{2,1,0:T(2,128)(2,1)S(1)} async-done(((bf16[32,1,48]{2,1,0:T(2,128)(2,1)}), bf16[32,1,48]{2,1,0:T(2,128)(2,1)S(1)}, u32[]{:S(2)}, u32[]{:S(2)}) %all-to-all-start.2) | async-done | bytes 3104 | tf_op jit(solution)/shard_map/all_to_all | solution.py:35
  182.1 0.7 reduce.3
  182.8 0.8 reshape.117
  183.7 7.2 %all-reduce.1 = (f32[128]{0:T(128)S(1)}, f32[128]{0:T(128)S(1)}) all-reduce(f32[128]{0:T(128)} %get-tuple-element.7, f32[128]{0:T(128)S(1)} %convolution_bitcast_fusion), channel_id=1, replica_groups=mesh['query'=4,'lib'=32] {'query'}, use_global_device_ids=true, to_apply=%region_7.8 | all-reduce | flops 256 | bytes 2048 | tf_op jit(solution)/shard_map/psum | solution.py:56
  190.9 1.3 log_add_fusion
  192.8 1.7 divide_convert_fusion
  (24 shorter events, 1.9 us)
Async XLA Ops:
  7.2 9.2 %copy-start = (bf16[768,2048]{1,0:T(8,128)(2,1)S(1)}, bf16[768,2048]{1,0:T(8,128)(2,1)}, u32[]{:S(2)}) copy-start(bf16[768,2048]{1,0:T(8,128)(2,1)} %param.7) | copy-start | bytes 9437188
  9.1 14.4 %all-to-all-start.1 = ((bf16[4,32,2048]{2,1,0:T(8,128)(2,1)}), bf16[4,32,2048]{2,1,0:T(8,128)(2,1)}, u32[]{:S(2)}, u32[]{:S(2)}) async-start(bf16[4,32,2048]{2,1,0:T(8,128)(2,1)} %stack.2), calls=%async_computation.1 | async-start | bytes 1048576 | tf_op jit(solution)/shard_map/all_to_all | solution.py:38
  23.5 10.8 %copy-start.3 = (u32[128]{0:T(128)S(1)}, u32[128]{0:T(128)}, u32[]{:S(2)}) copy-start(u32[128]{0:T(128)} %constant.75) | copy-start | bytes 1540
  23.5 12.0 %copy-start.2 = (s32[32]{0:T(128)S(1)}, s32[32]{0:T(128)}, u32[]{:S(2)}) copy-start(s32[32]{0:T(128)} %param.6) | copy-start | bytes 388
  23.5 117.5 %all-to-all-start = ((bf16[32,48,2048]{2,1,0:T(8,128)(2,1)}), bf16[32,48,2048]{2,1,0:T(8,128)(2,1)}, u32[]{:S(2)}, u32[]{:S(2)}) async-start(bf16[32,48,2048]{2,1,0:T(8,128)(2,1)} %bitcast.18), calls=%async_computation | async-start | bytes 12582912 | tf_op jit(solution)/shard_map/all_to_all | solution.py:32
  34.2 158.5 %reduce-scatter.2.cloned.1.call-start = ((), (), s32[]{:S(2)}) async-start(), calls=%async_computation.4 | async-start | bytes 1310720 | tf_op jit(solution)/shard_map/reduce_scatter | solution.py:57
  157.1 6.7 %copy-start.1 = (f32[128]{0:T(128)}, f32[128]{0:T(128)S(1)}, u32[]{:S(2)}) copy-start(f32[128]{0:T(128)S(1)} %pmax.7) | copy-start | bytes 1540
  166.1 16.0 %all-to-all-start.2 = ((bf16[32,1,48]{2,1,0:T(2,128)(2,1)}), bf16[32,1,48]{2,1,0:T(2,128)(2,1)S(1)}, u32[]{:S(2)}, u32[]{:S(2)}) async-start(bf16[32,1,48]{2,1,0:T(2,128)(2,1)} %all_to_all.16), calls=%async_computation.3 | async-start | bytes 32768 | tf_op jit(solution)/shard_map/all_to_all | solution.py:35
Sparse Core Ops, SparseCore 0:
  163.9 20.2 reduce-scatter.1
